TPU v7x, 512 devices: a whole 4x4x16 slice. The times are simulated.
512 devices in a mesh: row: 16 (over z), col: 32 (over y, x, core).
Axes of the slice: x: 4, y: 4, z: 16, core: 2. Of those that a mesh axis runs over, the one named last changes fastest.
Arguments:
- covariance: float32 [16384, 16384], P('row', 'col'), as said below
- fields: float32 [512, 16384], P('col', 'row'), may hold values from -6 to 6
Outputs:
- factored: float32 [16384, 16384], P('row', 'col')
- solved_fields: float32 [512, 16384], P('col', 'row')
Inputs may be any that keep to these rules, and one draw needn't show every extreme that they name: covariance, read in the global order of the steps, is symmetric positive definite.
All inputs are finite; a program needn't handle non-finite values.
Results may differ from a plain program's by a relative error of at most 0.0003.
Values sent between devices are 32-bit elements; how exact they have to be, the bound alone decides.
No kernel may reach another device: no remote copies, remote signals or barrier semaphores. Data moves between devices by JAX's collectives and lax.ppermute only.
A program may use at most 64 MiB of HBM per device.

v0:
```python
import jax
import jax.numpy as jnp
from jax import lax
from jax.sharding import PartitionSpec as P

NB = 512


PRECISE = lax.Precision.HIGHEST


def spread(block, axis, holder):
    block = jnp.where(lax.axis_index(axis) == holder, block, jnp.zeros_like(block))
    return lax.psum(block, axis)


def global_index(count, block, groups, index):
    local = jnp.arange(count, dtype=jnp.int32)
    return (local // block * groups + index) * block + local % block


def contract(left, right):
    return lax.dot_general(
        left, right, (((1,), (1,)), ((), ())), precision=PRECISE, preferred_element_type=jnp.float32
    )


def diagonal_block(matrix, field_local, step, block, ratio):
    row_count = lax.axis_size("row")
    stripe = ratio * block
    upper = step * stripe
    corner = matrix[upper : upper + stripe, step * block : (step + 1) * block]
    field_strip = field_local[:, upper : upper + stripe]
    width_fields = field_local.shape[0]
    across = lax.all_gather(corner, "col", axis=1, tiled=True)
    stacked, gathered = (
        lax.all_gather(across, "row", axis=0, tiled=True),
        lax.all_gather(field_strip, "row", axis=1, tiled=True),
    )
    square = stacked.reshape(row_count, ratio, block, NB).transpose(1, 0, 2, 3).reshape(NB, NB)
    gathered = (
        gathered.reshape(width_fields, row_count, ratio, block)
        .transpose(0, 2, 1, 3)
        .reshape(width_fields, NB)
    )
    factor = jnp.linalg.cholesky(square)
    inverse = jax.scipy.linalg.solve_triangular(factor, jnp.eye(NB, dtype=jnp.float32), lower=True)
    return (factor, inverse, gathered)


def factor_step(matrix, field_local, step, global_rows, block, ratio):
    row_count = lax.axis_size("row")
    row_index = lax.axis_index("row")
    column_index = lax.axis_index("col")
    local_rows = matrix.shape[0]
    width_fields = field_local.shape[0]
    stripe = ratio * block
    upper = step * stripe
    lower_bound = step * NB
    upper_bound = lower_bound + NB
    factor, inverse, gathered = diagonal_block(matrix, field_local, step, block, ratio)
    local_panel = matrix[:, step * block : (step + 1) * block]
    product = contract(lax.all_gather(local_panel, "col", axis=1, tiled=True), inverse)
    own_factor = lax.dynamic_index_in_dim(
        factor.reshape(ratio, row_count, block, NB), row_index, 1, keepdims=False
    )
    column = jnp.where(global_rows[:, None] < lower_bound, 0.0, product)
    column = column.at[upper : upper + stripe].set(own_factor.reshape(stripe, NB))
    trail = jnp.where(global_rows[:, None] >= upper_bound, column, 0.0)
    picked = lax.dynamic_index_in_dim(
        trail.reshape(local_rows // stripe, ratio, block, NB),
        column_index // row_count,
        1,
        keepdims=False,
    )
    transposed = spread(picked.reshape(local_rows // ratio, NB), "row", column_index % row_count)
    solved = contract(gathered, inverse)
    field_local = field_local - contract(solved, trail)
    own_solved = lax.dynamic_index_in_dim(
        solved.reshape(width_fields, ratio, row_count, block), row_index, 2, keepdims=False
    )
    field_local = field_local.at[:, upper : upper + stripe].set(
        own_solved.reshape(width_fields, stripe)
    )
    edge = lax.dynamic_slice_in_dim(column, column_index * block, block, 1)
    return (trail, transposed, field_local, edge)


def update(matrix, trail, transposed, first, last):
    return matrix.at[:, first:last].add(-contract(trail, transposed[first:last]))


def shards(covariance, fields):
    row_count = lax.axis_size("row")
    column_count = lax.axis_size("col")
    local_rows, local_columns = covariance.shape
    block = NB // column_count
    ratio = column_count // row_count
    global_rows = global_index(local_rows, block, row_count, lax.axis_index("row"))
    trail, transposed, field_local, edge_first = factor_step(
        covariance, fields, 0, global_rows, block, ratio
    )
    matrix = update(covariance, trail, transposed, block, local_columns)
    trail_next, transposed_next, field_local, edge_next = factor_step(
        matrix, field_local, 1, global_rows, block, ratio
    )
    matrix = update(matrix, trail_next, transposed_next, 2 * block, local_columns)
    remainder = jnp.where(global_rows[:, None] < 2 * NB, 0.0, matrix[:, 2 * block :])
    factored = jnp.concatenate([edge_first, edge_next, remainder], axis=1)
    return (factored, field_local)


def solution(mesh):
    return jax.shard_map(
        shards,
        mesh=mesh,
        in_specs=(P("row", "col"), P("col", "row")),
        out_specs=(P("row", "col"), P("col", "row")),
        check_vma=False,
    )
```

profile of v0, /device:TPU:2, one launch (start us, length us, event | category | flops | bytes accessed | tf_op | source)
XLA Modules:
  0.0 817.7 jit_solution(3939977811398627550)
XLA Ops:
  8.1 27.7 %all_gather.24 = f32[32,512]{0,1:T(8,128)S(1)} all-gather(f32[32,16]{0,1:T(8,128)S(1)} %copy.74), channel_id=1, replica_groups=mesh['row'=16,'col'=32] {'col'}, dimensions={1}, use_global_device_ids=true | all-gather | bytes 67584 | tf_op jit(solution)/shard_map/all_gather | solution.py:35
  37.6 69.5 %all-gather.7.cloned.1.call-done = f32[512,512]{1,0:T(8,128)} async-done(((f32[32,512]{1,0:T(8,128)}), f32[512,512]{1,0:T(8,128)}) %all-gather.7.cloned.1.call-update) | async-done | bytes 1048592 | tf_op jit(solution)/shard_map/all_gather | solution.py:37
  107.1 1.3 copy.53
  110.0 11.7 %cholesky.286 = f32[128,128]{1,0:T(8,128)S(1)} custom-call(f32[128,128]{1,0:T(8,128)S(1)} %cholesky.426), custom_call_target="Cholesky" | custom-call | tf_op jit(solution)/shard_map/jit(cholesky)/cholesky | solution.py:46
  121.7 9.8 %custom-call.27 = f32[1,128,128]{1,2,0:T(8,128)S(1)} custom-call(f32[1,128,128]{2,1,0:T(8,128)S(1)} %get-tuple-element.143), custom_call_target="InvertDiagBlocksLowerTriangular" | custom-call | tf_op jit(solution)/shard_map/jit(cholesky)/cholesky | solution.py:46
  132.9 1.3 convolution_subtract_fusion.7
  134.2 11.7 %cholesky.305 = f32[128,128]{1,0:T(8,128)S(1)} custom-call(f32[128,128]{1,0:T(8,128)S(1)} %cholesky.430), custom_call_target="Cholesky" | custom-call | tf_op jit(solution)/shard_map/jit(cholesky)/cholesky | solution.py:46
  145.9 10.2 %custom-call.28 = f32[1,128,128]{1,2,0:T(8,128)S(1)} custom-call(f32[1,128,128]{2,1,0:T(8,128)S(1)} %get-tuple-element.140), custom_call_target="InvertDiagBlocksLowerTriangular" | custom-call | tf_op jit(solution)/shard_map/jit(cholesky)/cholesky | solution.py:46
  156.5 1.3 convolution_subtract_fusion.9
  157.8 11.7 %cholesky.326 = f32[128,128]{1,0:T(8,128)S(1)} custom-call(f32[128,128]{1,0:T(8,128)S(1)} %cholesky.435), custom_call_target="Cholesky" | custom-call | tf_op jit(solution)/shard_map/jit(cholesky)/cholesky | solution.py:46
  169.5 9.8 %custom-call.29 = f32[1,128,128]{1,2,0:T(8,128)S(1)} custom-call(f32[1,128,128]{2,1,0:T(8,128)S(1)} %get-tuple-element.137), custom_call_target="InvertDiagBlocksLowerTriangular" | custom-call | tf_op jit(solution)/shard_map/jit(cholesky)/cholesky | solution.py:46
  180.8 11.7 %cholesky.343 = f32[128,128]{1,0:T(8,128)S(1)} custom-call(f32[128,128]{1,0:T(8,128)S(1)} %convolution_subtract_fusion.13), custom_call_target="Cholesky" | custom-call | tf_op jit(solution)/shard_map/jit(cholesky)/cholesky | solution.py:46
  198.4 7.8 while.10
  199.1 1.3 bitcast_dynamic-update-slice_fusion.4
  201.0 1.3 bitcast_dynamic-update-slice_fusion.4
  203.0 1.3 bitcast_dynamic-update-slice_fusion.4
  204.9 1.3 bitcast_dynamic-update-slice_fusion.4
  206.3 39.3 %custom-call.30 = f32[4,128,128]{1,2,0:T(8,128)S(1)} custom-call(f32[4,128,128]{2,1,0:T(8,128)S(1)} %get-tuple-element.90), custom_call_target="InvertDiagBlocksLowerTriangular" | custom-call | tf_op jit(solution)/shard_map/jit(_solve_triangular)/triangular_solve | solution.py:47
  251.2 5.4 select_bitcast_fusion
  256.6 2.3 scatter.14
  259.0 1.3 copy-done
  260.3 1.8 broadcast_select_fusion.1
  262.1 1.8 copy.59
  263.9 2.4 dynamic-slice_select_fusion.1
  266.6 3.5 slice.220
  270.1 2.9 copy.77
  273.0 129.6 %all-reduce.4.cloned.1.call-done = f32[512,512]{1,0:T(8,128)} async-done(((f32[512,512]{1,0:T(8,128)}), f32[512,512]{1,0:T(8,128)}) %all-reduce.4.cloned.1.call-update) | async-done | bytes 1048592 | tf_op jit(solution)/shard_map/psum | solution.py:14
  402.6 5.4 negate_add_fusion
  408.0 1.3 copy-done.1
  409.3 26.7 %all_gather.28 = f32[32,512]{0,1:T(8,128)} all-gather(f32[32,16]{0,1:T(8,128)S(1)} %slice.245), channel_id=1, replica_groups=mesh['row'=16,'col'=32] {'col'}, dimensions={1}, use_global_device_ids=true | all-gather | bytes 67584 | tf_op jit(solution)/shard_map/all_gather | solution.py:35
  436.0 1.7 copy.60
  438.5 29.0 %all-gather = f32[16,32,16]{1,2,0:T(8,128)S(1)} all-gather(f32[1,32,16]{1,2,0:T(8,128)S(1)} %slice_bitcast_fusion.17), channel_id=1, replica_groups=mesh['row'=16,'col'=32] {'row'}, dimensions={0}, use_global_device_ids=true | all-gather | bytes 34816 | tf_op jit(solution)/shard_map/all_gather | solution.py:38
  468.3 1.8 reshape.296
  470.1 1.7 copy.83
  474.3 2.1 fusion.20
  476.7 1.9 convolution_subtract_fusion.11
  479.6 26.8 %all-gather.1 = f32[16,32,16]{1,2,0:T(8,128)S(1)} all-gather(f32[1,32,16]{1,2,0:T(8,128)S(1)} %slice_bitcast_fusion.16), channel_id=1, replica_groups=mesh['row'=16,'col'=32] {'row'}, dimensions={0}, use_global_device_ids=true | all-gather | bytes 34816 | tf_op jit(solution)/shard_map/all_gather | solution.py:38
  507.7 1.5 slice.244
  509.7 1.3 copy.61
  512.6 11.7 %cholesky.358 = f32[128,128]{1,0:T(8,128)S(1)} custom-call(f32[128,128]{1,0:T(8,128)S(1)} %cholesky.439), custom_call_target="Cholesky" | custom-call | tf_op jit(solution)/shard_map/jit(cholesky)/cholesky | solution.py:46
  524.3 9.8 %custom-call.31 = f32[1,128,128]{1,2,0:T(8,128)S(1)} custom-call(f32[1,128,128]{2,1,0:T(8,128)S(1)} %get-tuple-element.133), custom_call_target="InvertDiagBlocksLowerTriangular" | custom-call | tf_op jit(solution)/shard_map/jit(cholesky)/cholesky | solution.py:46
  535.5 1.3 convolution_subtract_fusion.6
  536.8 11.7 %cholesky.377 = f32[128,128]{1,0:T(8,128)S(1)} custom-call(f32[128,128]{1,0:T(8,128)S(1)} %cholesky.443), custom_call_target="Cholesky" | custom-call | tf_op jit(solution)/shard_map/jit(cholesky)/cholesky | solution.py:46
  548.5 10.0 %custom-call.32 = f32[1,128,128]{1,2,0:T(8,128)S(1)} custom-call(f32[1,128,128]{2,1,0:T(8,128)S(1)} %get-tuple-element.130), custom_call_target="InvertDiagBlocksLowerTriangular" | custom-call | tf_op jit(solution)/shard_map/jit(cholesky)/cholesky | solution.py:46
  558.8 1.3 convolution_subtract_fusion.8
  560.1 11.7 %cholesky.398 = f32[128,128]{1,0:T(8,128)S(1)} custom-call(f32[128,128]{1,0:T(8,128)S(1)} %cholesky.448), custom_call_target="Cholesky" | custom-call | tf_op jit(solution)/shard_map/jit(cholesky)/cholesky | solution.py:46
  571.8 9.8 %custom-call.33 = f32[1,128,128]{1,2,0:T(8,128)S(1)} custom-call(f32[1,128,128]{2,1,0:T(8,128)S(1)} %get-tuple-element.127), custom_call_target="InvertDiagBlocksLowerTriangular" | custom-call | tf_op jit(solution)/shard_map/jit(cholesky)/cholesky | solution.py:46
  583.7 11.7 %cholesky.415 = f32[128,128]{1,0:T(8,128)S(1)} custom-call(f32[128,128]{1,0:T(8,128)S(1)} %convolution_subtract_fusion.12), custom_call_target="Cholesky" | custom-call | tf_op jit(solution)/shard_map/jit(cholesky)/cholesky | solution.py:46
  601.4 7.9 while.11
  602.1 1.3 bitcast_dynamic-update-slice_fusion.5
  604.0 1.3 bitcast_dynamic-update-slice_fusion.5
  606.0 1.3 bitcast_dynamic-update-slice_fusion.5
  608.0 1.3 bitcast_dynamic-update-slice_fusion.5
  609.3 39.3 %custom-call.34 = f32[4,128,128]{1,2,0:T(8,128)S(1)} custom-call(f32[4,128,128]{2,1,0:T(8,128)S(1)} %get-tuple-element.91), custom_call_target="InvertDiagBlocksLowerTriangular" | custom-call | tf_op jit(solution)/shard_map/jit(_solve_triangular)/triangular_solve | solution.py:47
  651.4 1.3 fusion.48
  653.4 1.3 fusion.47
  654.7 6.4 convolution_select_fusion
  661.1 2.1 scatter.15
  663.2 1.8 broadcast_select_fusion
  665.0 1.8 copy.66
  666.8 2.4 dynamic-slice_select_fusion
  674.6 128.6 %all-reduce.6.cloned.1.call-done = f32[512,512]{1,0:T(8,128)} async-done(((f32[512,512]{1,0:T(8,128)}), f32[512,512]{1,0:T(8,128)}) %all-reduce.6.cloned.1.call-update) | async-done | bytes 1048592 | tf_op jit(solution)/shard_map/psum | solution.py:14
  803.2 5.2 fusion
  808.6 1.8 copy.72
  (151 shorter events, 46.1 us)
Async XLA Ops:
  7.2 29.4 %slice-start = ((f32[1024,512]{1,0:T(8,128)}), f32[1024,16]{1,0:T(8,128)S(1)}, s32[]{:S(2)}) async-start(f32[1024,512]{1,0:T(8,128)} %param.17), calls=%async_computation.6 | async-start | bytes 1048576 | tf_op jit(solution)/shard_map/slice | solution.py:62
  7.2 99.9 %all-gather.7.cloned.1.call-start = ((), (), s32[]{:S(2)}) async-start(), calls=%async_computation | async-start | bytes 1114112 | tf_op jit(solution)/shard_map/all_gather | solution.py:37
  36.5 214.7 %all-gather.9.cloned.1.call-start = ((), (), s32[]{:S(2)}) async-start(), calls=%async_computation.1 | async-start | bytes 2162688 | tf_op jit(solution)/shard_map/all_gather | solution.py:63
  37.4 365.2 %all-reduce.4.cloned.1.call-start = ((), (), s32[]{:S(2)}) async-start(), calls=%async_computation.2 | async-start | bytes 2097152 | tf_op jit(solution)/shard_map/psum | solution.py:14
  109.0 1.0 copy-start.5
  248.5 0.9 copy-start.2
  249.4 0.7 copy-start.7
  259.0 1.4 copy-start
  266.3 243.4 %all-gather.13.cloned.1.call-start = ((), (), s32[]{:S(2)}) async-start(), calls=%async_computation.4 | async-start | bytes 1114112 | tf_op jit(solution)/shard_map/all_gather | solution.py:37
  407.9 1.3 copy-start.1
  437.7 216.9 %all-gather.11.cloned.1.call-start = ((), (), s32[]{:S(2)}) async-start(), calls=%async_computation.3 | async-start | bytes 2162688 | tf_op jit(solution)/shard_map/all_gather | solution.py:63
  509.2 293.9 %all-reduce.6.cloned.1.call-start = ((), (), s32[]{:S(2)}) async-start(), calls=%async_computation.5 | async-start | bytes 2097152 | tf_op jit(solution)/shard_map/psum | solution.py:14
  511.6 1.0 copy-start.6
  648.7 1.9 copy-start.10
  651.0 10.1 %copy-start.3 = (f32[128,512]{1,0:T(8,128)}, f32[128,512]{1,0:T(8,128)S(1)}, u32[]{:S(2)}) copy-start(f32[128,512]{1,0:T(8,128)S(1)} %fusion.50) | copy-start | bytes 786436
  652.7 8.4 %copy-start.8 = (f32[128,512]{1,0:T(8,128)}, f32[128,512]{1,0:T(8,128)S(1)}, u32[]{:S(2)}) copy-start(f32[128,512]{1,0:T(8,128)S(1)} %fusion.48) | copy-start | bytes 786436
  666.8 3.3 copy-start.4
  666.8 3.3 copy-start.9
  666.8 3.3 copy-start.12
  673.7 134.7 %copy-start.11 = (f32[16,1024]{1,0:T(8,128)}, f32[16,1024]{1,0:T(8,128)S(1)}, u32[]{:S(2)}) copy-start(f32[16,1024]{1,0:T(8,128)S(1)} %scatter.19) | copy-start | bytes 196612
Sparse Core Ops, SparseCore 0:
  36.6 70.4 all-gather.6
  110.8 55.8 all-gather.8
  266.4 136.0 all-reduce.3
  437.8 65.6 all-gather.12
  509.4 53.8 all-gather.10
  669.4 133.7 all-reduce.5
where the time goes:
time: 829 us; the launch traced here: 818 us
  waiting for transfers between devices  328 us (40%)
  other arithmetic  251 us (30%)
  blocking collectives  110 us (13%)
  local copies, waits for them, and re-layouts  59.1 us (7%)
  matrix products  48.1 us (6%)
  between operations  20.6 us (2%)
    psum x2, waiting for transfers between devices, spread(): return lax.psum(block, axis)  258 us
    another operation x29, other arithmetic, diagonal_block(): factor = jnp.linalg.cholesky(square)  158 us
    another operation x5, other arithmetic, diagonal_block(): jax.scipy.linalg.solve_triangular(factor, jnp.eye(NB, dtype=jnp.float32),...  81.1 us
    all_gather x2, waiting for transfers between devices, diagonal_block(): lax.all_gather(across, 'row', axis=0, tiled=True)  69.5 us
    all_gather x2, blocking collectives, diagonal_block(): lax.all_gather(field_strip, 'row', axis=1, tiled=True)  55.8 us
    all_gather x2, blocking collectives, diagonal_block(): across = lax.all_gather(corner, 'col', axis=1, tiled=True)  54.3 us
    dot_general x8, matrix products, contract(): lax.dot_general(left, right, (((1,), (1,)), ((), ())), precision=PRECISE,...  28.5 us
  transfers between devices with their start and end apart: 6, of which 3 were waited for; matrix products, arithmetic and copies ran while one was open for 38% of the time, Pallas kernels for 0%

commit v1 on v0

v1 whole, which is shorter than its diff:
```python
import functools

import jax
import jax.numpy as jnp
from jax import lax
from jax.experimental import pallas as pl
from jax.experimental.pallas import tpu as pltpu
from jax.sharding import PartitionSpec as P

F32 = jnp.float32
BF16 = jnp.bfloat16
HI = lax.Precision.HIGHEST
NB = 512
WIDE = 2 * NB


def mm(a, b):
    return lax.dot_general(a, b, (((1,), (0,)), ((), ())), precision=HI, preferred_element_type=F32)

def tmm(a, b):
    return lax.dot_general(a, b, (((0,), (0,)), ((), ())), precision=HI, preferred_element_type=F32)

def eliminate(t, out_ref, rows=32, size=128):
    lane = lax.broadcasted_iota(jnp.int32, (8, size), 1)
    sub = lax.broadcasted_iota(jnp.int32, (8, size), 0)
    nv = rows // 8
    for p in range(size // rows):
        k0 = p * rows
        R = [t[8 * v:8 * v + 8, :] for v in range(nv)]
        for s in range(nv):
            c0 = k0 + 8 * s
            inside = (lane >= c0) & (lane < c0 + 8)
            B = [[None] * nv for _ in range(8)]
            for j in range(8):
                for v in range(s, nv):
                    B[j][v] = jnp.broadcast_to(R[v][:, c0 + j:c0 + j + 1], (8, size))
            R[s] = jnp.where(inside, jnp.where(lane - c0 == sub, 1.0, 0.0), R[s])
            for v in range(s + 1, nv):
                R[v] = jnp.where(inside, 0.0, R[v])
            scale = jnp.zeros((8, size), F32)
            for j in range(8):
                d = jnp.broadcast_to(B[j][s][j:j + 1, :], (8, size))
                scale = jnp.where(sub == j, d, scale)
                inv = 1.0 / d
                bl = [None] * 8
                for l in range(j + 1, 8):
                    bl[l] = jnp.broadcast_to(B[l][s][j:j + 1, :], (8, size))
                r = jnp.broadcast_to(R[s][j:j + 1, :], (8, size))
                for v in range(s, nv):
                    m = B[j][v] * inv
                    if v == s:
                        m = jnp.where(sub > j, m, 0.0)
                    for l in range(j + 1, 8):
                        B[l][v] = B[l][v] - m * bl[l]
                    R[v] = R[v] - m * r
            R[s] = R[s] * (1.0 / jnp.sqrt(scale))
        panel = jnp.concatenate(R, axis=0) if nv > 1 else R[0]
        out_ref[k0:k0 + rows, :] = panel
        k1 = k0 + rows
        if k1 < size:
            lane_r = lax.broadcasted_iota(jnp.int32, (rows, size), 1)
            rest = t[rows:, :]
            lr = lax.broadcasted_iota(jnp.int32, rest.shape, 1)
            rest = jnp.where((lr >= k0) & (lr < k1), 0.0, rest)
            sub_r = lax.broadcasted_iota(jnp.int32, (rows, size), 0)
            right = jnp.where((lane_r < k1) & (lane_r - k0 > sub_r), 0.0, panel)
            up = tmm(panel, right)
            t = rest - up[k1:, :]

def factor_kernel(at_ref, own_ref, other_ref, w_ref, w2, rbuf, blk):
    nb = 256
    steps = WIDE // nb
    chips, block, _ = own_ref.shape
    core = at_ref[1] % 2
    for ref, side in ((own_ref, core), (other_ref, 1 - core)):
        for c in range(chips):
            lo = pl.multiple_of((2 * c + side) * block, block)
            w_ref[pl.ds(lo, block), :] = ref[c, :, 0:WIDE]
            w_ref[pl.ds(NB + lo, block), NB:WIDE] = ref[c, :, WIDE : WIDE + NB]
    w_ref[NB:WIDE, 0:NB] = jnp.zeros((NB, NB), F32)
    tri = (lax.broadcasted_iota(jnp.int32, (128, 128), 0) >= lax.broadcasted_iota(jnp.int32, (128, 128), 1))

    def outer(k, _):
        o = pl.multiple_of(k * nb, nb)
        oa, ob = pl.ds(o, 128), pl.ds(pl.multiple_of(o + 128, 128), 128)
        eliminate(w_ref[oa, oa], blk)
        waa = jnp.where(tri, blk[...], 0.0)
        w2[0:128, 0:128] = waa
        w2[0:128, 128:256] = jnp.zeros((128, 128), F32)
        uab = mm(waa, w_ref[oa, ob])
        vba = -tmm(uab, waa)
        eliminate(w_ref[ob, ob] - tmm(uab, uab), blk)
        wbb = jnp.where(tri, blk[...], 0.0)
        w2[128:256, 128:256] = wbb
        w2[128:256, 0:128] = mm(wbb, vba)
        row = pl.ds(o, nb)

        def scale(c, _):
            col = pl.ds(pl.multiple_of(c * nb, nb), nb)

            @pl.when(c != k)
            def _():
                rbuf[:, col] = mm(w2[...], w_ref[row, col])

            @pl.when(c == k)
            def _():
                rbuf[:, col] = w2[...]

            @pl.when(c <= k)
            def _():
                w_ref[row, col] = rbuf[:, col]

            @pl.when(c > k)
            def _():
                w_ref[row, col] = jnp.zeros((nb, nb), F32)
            return 0

        lax.fori_loop(0, steps, scale, 0)

        def below(j, _):
            jo = pl.ds(pl.multiple_of(j * nb, nb), nb)

            def one(c, _):
                col = pl.ds(pl.multiple_of(c * nb, nb), nb)

                @pl.when((c < k) | (c >= j))
                def _():
                    w_ref[jo, col] = w_ref[jo, col] - tmm(rbuf[:, jo], rbuf[:, col])

                @pl.when(c == k)
                def _():
                    w_ref[jo, col] = -tmm(rbuf[:, jo], rbuf[:, col])
                return 0

            lax.fori_loop(0, steps, one, 0)
            return 0

        lax.fori_loop(k + 1, steps, below, 0)
        return 0

    lax.fori_loop(0, steps, outer, 0)

def inverse_factor(at, own, other):
    vmem = pl.BlockSpec(memory_space=pltpu.VMEM)
    return pl.pallas_call(
        factor_kernel,
        out_shape=jax.ShapeDtypeStruct((WIDE, WIDE), F32),
        in_specs=[pl.BlockSpec(memory_space=pltpu.SMEM), vmem, vmem],
        out_specs=vmem,
        scratch_shapes=[pltpu.VMEM((256, 256), F32), pltpu.VMEM((256, WIDE), F32), pltpu.VMEM((128, 128), F32)],
        compiler_params=pltpu.CompilerParams(vmem_limit_bytes=24 << 20),
        cost_estimate=pl.CostEstimate(flops=8_000_000_000, bytes_accessed=8 << 20, transcendentals=0),
        name="inverse_factor",
    )(at, own, other)


def split(x):
    high = x.astype(BF16)
    return high, (x - high.astype(F32)).astype(BF16)


def column_kernel(w_ref, g_ref, high_ref, low_ref, y_ref, a_ref):
    groups, top, wide = g_ref.shape
    block = 16
    size = groups * block
    for q in range(top // block):
        a_ref[q * size : (q + 1) * size, :] = g_ref[:, q * block : (q + 1) * block, :].reshape(size, wide)
    for i in range(0, WIDE, size):
        z = mm(w_ref[i : i + size, : i + size], a_ref[: i + size, :])
        high_ref[i : i + size, :], low_ref[i : i + size, :] = split(z)
        y_ref[i : i + size, :] = z[:, wide - 128 :]


def column_part(w, gathered):
    vmem = pl.BlockSpec(memory_space=pltpu.VMEM)
    wide = gathered.shape[2]
    return pl.pallas_call(
        column_kernel,
        out_shape=(
            jax.ShapeDtypeStruct((WIDE, wide), BF16),
            jax.ShapeDtypeStruct((WIDE, wide), BF16),
            jax.ShapeDtypeStruct((WIDE, 128), F32),
        ),
        in_specs=[vmem, vmem],
        out_specs=(vmem, vmem, vmem),
        scratch_shapes=[pltpu.VMEM((WIDE, wide), F32)],
        compiler_params=pltpu.CompilerParams(vmem_limit_bytes=24 << 20),
        cost_estimate=pl.CostEstimate(flops=6_000_000_000, bytes_accessed=8 << 20, transcendentals=0),
        name="column_part",
    )(w, gathered)


def row_kernel(at_ref, w_ref, high_ref, low_ref, g_ref, cov_ref, field_ref, out_ref, fout_ref, p_ref, x_ref):
    column_groups, _, block, tile = g_ref.shape
    row_groups = 16
    columns = cov_ref.shape[1]
    width = field_ref.shape[0]
    size = 256
    own = 2 * block
    for p in range(2):
        p_ref[p * NB : (p + 1) * NB, :] = g_ref[:, p].reshape(NB, tile)
    for i in range(0, WIDE, size):
        x_ref[i : i + size, :] = mm(w_ref[i : i + size, : i + size], p_ref[: i + size, :])
    x_high, x_low = split(x_ref[...].T)
    z_high, z_low = high_ref[...], low_ref[...]

    def dot(a, b):
        return jnp.dot(a, b, preferred_element_type=F32)

    change = dot(x_high, z_high) + (dot(x_high, z_low) + dot(x_low, z_high))
    local = lax.broadcasted_iota(jnp.int32, (tile, 1), 0) + pl.program_id(0) * tile
    rows = (local // block * row_groups + at_ref[0]) * block + local % block
    mine = pl.multiple_of(at_ref[1] * block, block)
    edge = jnp.concatenate([x_ref[pl.ds(mine, block), :], x_ref[pl.ds(NB + mine, block), :]], axis=0).T
    lane = lax.broadcasted_iota(jnp.int32, (1, own), 1)
    lanes = (lane // block * column_groups + at_ref[1]) * block + lane % block
    out_ref[...] = jnp.where(rows < WIDE, 0.0, cov_ref[...] - change[:, :columns])
    out_ref[:, :own] = jnp.where(rows >= lanes, edge, 0.0)
    fout_ref[...] = field_ref[...] - change[:, columns:].T[:width]


def row_part(at, w, high, low, gathered, covariance, fields):
    vmem = pl.BlockSpec(memory_space=pltpu.VMEM)
    tile = 256
    groups, _, block, local_rows = gathered.shape
    columns = covariance.shape[1]
    width = fields.shape[0]
    return pl.pallas_call(
        row_kernel,
        grid=(local_rows // tile,),
        out_shape=(
            jax.ShapeDtypeStruct(covariance.shape, F32),
            jax.ShapeDtypeStruct(fields.shape, F32),
        ),
        in_specs=[
            pl.BlockSpec(memory_space=pltpu.SMEM),
            vmem,
            vmem,
            vmem,
            pl.BlockSpec((groups, 2, block, tile), lambda i: (0, 0, 0, i)),
            pl.BlockSpec((tile, columns), lambda i: (i, 0)),
            pl.BlockSpec((width, tile), lambda i: (0, i)),
        ],
        out_specs=(
            pl.BlockSpec((tile, columns), lambda i: (i, 0)),
            pl.BlockSpec((width, tile), lambda i: (0, i)),
        ),
        scratch_shapes=[pltpu.VMEM((WIDE, tile), F32), pltpu.VMEM((WIDE, tile), F32)],
        compiler_params=pltpu.CompilerParams(vmem_limit_bytes=40 << 20),
        cost_estimate=pl.CostEstimate(flops=12_000_000_000, bytes_accessed=16 << 20, transcendentals=0),
        name="row_part",
    )(at, w, high, low, gathered, covariance, fields)


def spread_out(piece, axis, count, groups=None):
    copies = jnp.broadcast_to(piece[None], (count,) + piece.shape)
    return lax.all_to_all(copies, axis, 0, 0, axis_index_groups=groups, tiled=True)


def finish(at, covariance, fields, own_pieces, other_pieces, panel, across):
    width = fields.shape[0]
    w = inverse_factor(at, own_pieces, other_pieces)
    high, low, y = column_part(w, across)
    factored, moved = row_part(at, w, high, low, panel, covariance, fields)
    row_groups, top, _ = across.shape
    block = WIDE // row_groups // (top // 16)
    solved = y.reshape(top // block, row_groups, block, 128)
    solved = lax.dynamic_index_in_dim(solved, at[0], 1, keepdims=False).reshape(top, 128)[:, :width]
    return (factored, moved.at[:, :top].set(solved.T))


def shards(covariance, fields):
    rows_n = lax.axis_size("row")
    cols_n = lax.axis_size("col")
    at = jnp.stack([lax.axis_index("row"), lax.axis_index("col")]).astype(jnp.int32)
    local_rows, local_columns = covariance.shape
    width = fields.shape[0]
    block = NB // cols_n
    top = WIDE // rows_n
    own = 2 * block
    quarters = top // block
    cores = 2

    corner = covariance[:top, :own]
    packed = jnp.concatenate([corner[q * block : (q + 1) * block] for q in range(quarters)], axis=1)
    tall = spread_out(packed, "row", rows_n).reshape(rows_n * block, quarters * own).T
    strip = jnp.concatenate([tall[q * own : (q + 1) * own] for q in range(quarters)], axis=1)
    strip = jnp.concatenate([strip[:block], strip[block:, NB:]], axis=1)
    same_core = [[cores * i + k for i in range(cols_n // cores)] for k in range(cores)]
    own_pieces = spread_out(strip, "col", cols_n // cores, same_core)
    other_pieces = lax.ppermute(own_pieces, "col", [(i, i ^ 1) for i in range(cols_n)])

    across = jnp.concatenate([covariance[:top], jnp.pad(fields[:, :top].T, ((0, 0), (0, 128 - width)))], axis=1)
    across = lax.all_gather(across, "row", axis=0)
    panel = covariance[:, :own].T.reshape(2, block, local_rows)
    panel = lax.all_gather(panel, "col", axis=0)
    return finish(at, covariance, fields, own_pieces, other_pieces, panel, across)


def solution(mesh):
    return jax.shard_map(
        shards,
        mesh=mesh,
        in_specs=(P("row", "col"), P("col", "row")),
        out_specs=(P("row", "col"), P("col", "row")),
        check_vma=False,
    )
```

time: 829 us -> 190 us (0.23)
  the two profiles are of different devices: /device:TPU:2 before, /device:TPU:1 now
where the time goes in v1:
time: 190 us; the launch traced here: 189 us
  Pallas kernels  77.8 us (41%)
  blocking collectives  53 us (28%)
  local copies, waits for them, and re-layouts  21.5 us (11%)
  between operations  14.1 us (7%)
  waiting for transfers between devices  13.2 us (7%)
  starting transfers between devices  6.83 us (4%)
  other arithmetic  2.89 us (2%)
    all_to_all x2, blocking collectives, spread_out(): lax.all_to_all(copies, axis, 0, 0, axis_index_groups=groups, tiled=True)  53 us
    pallas_call x1, Pallas kernels, inverse_factor(): pl.pallas_call(factor_kernel, out_shape=jax.ShapeDtypeStruct((WIDE, WIDE)...  50.6 us
    pallas_call x1, Pallas kernels, row_part(): pl.pallas_call(row_kernel, grid=(local_rows // tile,), out_shape=(jax.Sha...  20.8 us
    unnamed x24, local copies, waits for them, and re-layouts  15.3 us
    all_gather x1, waiting for transfers between devices, shards(): panel = lax.all_gather(panel, 'col', axis=0)  11 us
    ppermute x1, starting transfers between devices, shards(): lax.ppermute(own_pieces, 'col', [(i, i ^ 1) for i in range(cols_n)])  6.75 us
    pallas_call x1, Pallas kernels, column_part(): pl.pallas_call(column_kernel, out_shape=(jax.ShapeDtypeStruct((WIDE, wide...  6.45 us
  transfers between devices with their start and end apart: 3, of which 2 were waited for; matrix products, arithmetic and copies ran while one was open for 2% of the time, Pallas kernels for 30%

profile of v1, /device:TPU:1, one launch (start us, length us, event | category | flops | bytes accessed | tf_op | source)
XLA Modules:
  0.0 189.4 jit_solution(17817596002384842460)
XLA Ops:
  7.2 0.0 all-gather.6.cloned.1.call-start
  7.2 0.9 slice.77
  8.1 0.7 slice_bitcast_fusion.1
  8.8 0.1 copy.25
  8.9 0.7 select_maximum_fusion
  9.6 0.0 all-gather.6.cloned.1.call-update
  9.6 0.0 all-gather.4.cloned.1.call-start
  9.7 1.1 slice_bitcast_fusion
  10.8 0.8 copy.20
  11.6 0.0 all-gather.4.cloned.1.call-update
  11.6 0.8 fusion.1
  12.4 0.1 pad_maximum_fusion.4
  12.4 27.5 %all_to_all.10 = f32[16,16,128]{2,1,0:T(8,128)S(1)} all-to-all(f32[16,16,128]{2,1,0:T(8,128)S(1)} %broadcast_in_dim.4), channel_id=1, replica_groups=mesh['row'=16,'col'=32] {'row'}, dimensions={0} | all-to-all | bytes 262144 | tf_op jit(solution)/shard_map/all_to_all | solution.py:257
  40.0 0.2 fusion.2
  40.1 0.1 copy.13
  40.2 0.1 copy.14
  40.3 0.1 copy.15
  40.4 0.1 copy.16
  40.5 0.2 broadcast_in_dim.5
  40.6 25.5 %all_to_all.11.own_ref = f32[16,16,1536]{2,1,0:T(8,128)S(1)} all-to-all(f32[16,16,1536]{2,1,0:T(8,128)S(1)} %broadcast_in_dim.5), channel_id=1, replica_groups={{0,2,4,6,8,10,12,14,16,18,20,22,24,26,28,30},{1,3,5,7,9,11,13,15,17,19,..., dimensions={0} | all-to-all | bytes 3145728 | tf_op jit(solution)/shard_map/all_to_all | solution.py:257
  66.1 6.8 %collective-permute-start = (f32[16,16,1536]{2,1,0:T(8,128)S(1)}, f32[16,16,1536]{2,1,0:T(8,128)S(1)}, u32[]{:S(2)}, u32[]{:S(2)}) collective-permute-start(f32[16,16,1536]{2,1,0:T(8,128)S(1)} %all_to_all.11.own_ref), channel_id=1, source_target_pairs={{0,1},{1,0},{2,3},{3,2},{4,5},{5,4},{6,7},{7,6},{8,9},{9,8},{10,11... | collective-permute-start | bytes 4718600 | tf_op jit(solution)/shard_map/ppermute | solution.py:291
  72.9 0.7 compare_reduce_fusion
  73.6 0.1 pad_add_fusion.at_ref
  73.7 2.2 %collective-permute-done.other_ref = f32[16,16,1536]{2,1,0:T(8,128)S(1)} collective-permute-done((f32[16,16,1536]{2,1,0:T(8,128)S(1)}, f32[16,16,1536]{2,1,0:T(8,128)S(1)}, u32[]{:S(2)}, u32[]{:S(2)}) %collective-permute-start) | collective-permute-done | bytes 1572896 | tf_op jit(solution)/shard_map/ppermute | solution.py:291
  75.9 50.6 %inverse_factor.1.w_ref = f32[1024,1024]{1,0:T(8,128)S(1)} custom-call(s32[2]{0:T(128)S(1)} %pad_add_fusion.at_ref, f32[16,16,1536]{2,1,0:T(8,128)S(1)} %all_to_all.11.own_ref, f32[16,16,1536]{2,1,0:T(8,128)S(1)} %collective-permute-done.other_ref), custom_call_target="tpu_custom_call" | custom-call | flops 8000000000 | bytes 8388608 | tf_op jit(solution)/shard_map/inverse_factor/pallas_call | solution.py:145
  126.5 0.0 copy-start.4
  126.5 2.0 %copy-done.4 = f32[1024,1024]{1,0:T(8,128)} copy-done((f32[1024,1024]{1,0:T(8,128)}, f32[1024,1024]{1,0:T(8,128)S(1)}, u32[]{:S(2)}) %copy-start.4) | copy-done | bytes 4194328
  128.5 0.0 all-gather.6.cloned.1.call-done
  128.5 0.0 copy-start.3
  128.5 1.7 copy-done.3
  130.2 0.0 copy-start.5
  130.2 2.2 %copy-done.5 = f32[1024,1024]{1,0:T(8,128)S(1)} copy-done((f32[1024,1024]{1,0:T(8,128)S(1)}, f32[1024,1024]{1,0:T(8,128)}, u32[]{:S(2)}) %copy-start.5) | copy-done | bytes 4194328
  132.4 0.0 copy-start
  132.4 0.0 copy-start.1
  132.4 6.4 %column_part.1 = (bf16[1024,640]{1,0:T(8,128)(2,1)S(1)}, bf16[1024,640]{1,0:T(8,128)(2,1)S(1)}, f32[1024,128]{1,0:T(8,128)S(1)}) custom-call(f32[1024,1024]{1,0:T(8,128)S(1)} %copy-done.5, f32[16,64,640]{2,1,0:T(8,128)S(1)} %bitcast.19), custom_call_target="tpu_custom_call" | custom-call | flops 6000000000 | bytes 8388608 | tf_op jit(solution)/shard_map/column_part/pallas_call | solution.py:177
  138.9 0.0 copy-start.7
  138.9 1.0 copy-done.7
  139.9 0.0 copy-start.9
  139.9 1.1 copy-done.9
  141.1 0.1 copy.24
  141.2 11.0 %all-gather.4.cloned.1.call-done.g_ref = f32[32,2,16,1024]{3,2,1,0:T(8,128)} async-done(((f32[1,2,16,1024]{3,2,1,0:T(8,128)}), f32[32,2,16,1024]{3,2,1,0:T(8,128)}) %all-gather.4.cloned.1.call-update) | async-done | bytes 4194320 | tf_op jit(solution)/shard_map/all_gather | solution.py:296
  152.1 0.0 copy-done
  152.1 0.0 copy-done.1
  152.1 0.0 copy-start.2
  152.1 2.2 %copy-done.2 = f32[32,2,16,1024]{3,2,1,0:T(8,128)S(1)} copy-done((f32[32,2,16,1024]{3,2,1,0:T(8,128)S(1)}, f32[32,2,16,1024]{3,2,1,0:T(8,128)}, u32[]{:S(2)}) %copy-start.2) | copy-done | bytes 4194328
  154.3 0.0 copy-start.6
  154.3 2.2 %copy-done.6 = f32[1024,1024]{1,0:T(8,128)S(1)} copy-done((f32[1024,1024]{1,0:T(8,128)S(1)}, f32[1024,1024]{1,0:T(8,128)}, u32[]{:S(2)}) %copy-start.6) | copy-done | bytes 4194328
  156.5 0.0 copy-start.8
  156.5 1.3 copy-done.8
  157.8 0.0 copy-start.10
  157.8 1.3 copy-done.10
  159.1 20.8 %row_part.1 = (f32[1024,512]{1,0:T(8,128)}, f32[16,1024]{1,0:T(8,128)}) custom-call(s32[2]{0:T(128)S(1)} %pad_add_fusion.at_ref, f32[1024,1024]{1,0:T(8,128)S(1)} %copy-done.6, bf16[1024,640]{1,0:T(8,128)(2,1)S(1)} %copy-done.8, bf16[1024,640]{1,0:T(8,128)(2,1)S(1)} %copy-done.10, f32[32,2,16,1024]{3,2,1,0:T(8,128)S(1)} %copy-done.2, ...), custom_call_target="tpu_custom_call" | custom-call | flops 12000000000 | bytes 16777216 | tf_op jit(solution)/shard_map/row_part/pallas_call | solution.py:228
  179.9 1.3 bitcast_select_fusion
  181.2 1.3 scatter.4
  (3 shorter events, 0.0 us)
Async XLA Ops:
  7.2 121.3 %all-gather.6.cloned.1.call-start = ((), (), s32[]{:S(2)}) async-start(), calls=%async_computation.3 | async-start | bytes 2785280 | tf_op jit(solution)/shard_map/all_gather | solution.py:294
  9.6 142.5 %all-gather.4.cloned.1.call-start = ((), (), s32[]{:S(2)}) async-start(), calls=%async_computation.2 | async-start | bytes 4325376 | tf_op jit(solution)/shard_map/all_gather | solution.py:296
  66.1 9.8 %collective-permute-start = (f32[16,16,1536]{2,1,0:T(8,128)S(1)}, f32[16,16,1536]{2,1,0:T(8,128)S(1)}, u32[]{:S(2)}, u32[]{:S(2)}) collective-permute-start(f32[16,16,1536]{2,1,0:T(8,128)S(1)} %all_to_all.11.own_ref), channel_id=1, source_target_pairs={{0,1},{1,0},{2,3},{3,2},{4,5},{5,4},{6,7},{7,6},{8,9},{9,8},{10,11... | collective-permute-start | bytes 4718600 | tf_op jit(solution)/shard_map/ppermute | solution.py:291
  126.5 2.0 %copy-start.4 = (f32[1024,1024]{1,0:T(8,128)}, f32[1024,1024]{1,0:T(8,128)S(1)}, u32[]{:S(2)}) copy-start(f32[1024,1024]{1,0:T(8,128)S(1)} %inverse_factor.1.w_ref) | copy-start | bytes 12582916
  128.5 1.7 copy-start.3
  130.2 2.2 %copy-start.5 = (f32[1024,1024]{1,0:T(8,128)S(1)}, f32[1024,1024]{1,0:T(8,128)}, u32[]{:S(2)}) copy-start(f32[1024,1024]{1,0:T(8,128)} %copy-done.4) | copy-start | bytes 12582916
  132.4 19.7 %copy-start = (f32[1024,512]{1,0:T(8,128)S(1)}, f32[1024,512]{1,0:T(8,128)}, u32[]{:S(2)}) copy-start(f32[1024,512]{1,0:T(8,128)} %cov_ref.1) | copy-start | bytes 6291460
  132.4 19.7 %copy-start.1 = (f32[16,1024]{1,0:T(8,128)S(1)}, f32[16,1024]{1,0:T(8,128)}, u32[]{:S(2)}) copy-start(f32[16,1024]{1,0:T(8,128)} %field_ref.1) | copy-start | bytes 196612
  138.9 1.1 copy-start.7
  139.9 1.2 copy-start.9
  152.1 2.2 %copy-start.2 = (f32[32,2,16,1024]{3,2,1,0:T(8,128)S(1)}, f32[32,2,16,1024]{3,2,1,0:T(8,128)}, u32[]{:S(2)}) copy-start(f32[32,2,16,1024]{3,2,1,0:T(8,128)} %all-gather.4.cloned.1.call-done.g_ref) | copy-start | bytes 12582916
  154.3 2.2 %copy-start.6 = (f32[1024,1024]{1,0:T(8,128)S(1)}, f32[1024,1024]{1,0:T(8,128)}, u32[]{:S(2)}) copy-start(f32[1024,1024]{1,0:T(8,128)} %copy-done.4) | copy-start | bytes 12582916
  156.5 1.3 copy-start.8
  157.8 1.3 copy-start.10
Sparse Core Ops, SparseCore 0:
  10.6 71.9 all-gather.5
  85.7 66.3 all-gather.3

commit v2 on v1

--- a/solution.py
+++ b/solution.py
@@ -148,7 +148,7 @@
         in_specs=[pl.BlockSpec(memory_space=pltpu.SMEM), vmem, vmem],
         out_specs=vmem,
         scratch_shapes=[pltpu.VMEM((256, 256), F32), pltpu.VMEM((256, WIDE), F32), pltpu.VMEM((128, 128), F32)],
-        compiler_params=pltpu.CompilerParams(vmem_limit_bytes=24 << 20),
+        compiler_params=pltpu.CompilerParams(vmem_limit_bytes=12 << 20),
         cost_estimate=pl.CostEstimate(flops=8_000_000_000, bytes_accessed=8 << 20, transcendentals=0),
         name="inverse_factor",
     )(at, own, other)
@@ -159,74 +159,110 @@
     return high, (x - high.astype(F32)).astype(BF16)
 
 
-def column_kernel(w_ref, g_ref, high_ref, low_ref, y_ref, a_ref):
-    groups, top, wide = g_ref.shape
-    block = 16
-    size = groups * block
-    for q in range(top // block):
-        a_ref[q * size : (q + 1) * size, :] = g_ref[:, q * block : (q + 1) * block, :].reshape(size, wide)
+def panel_kernel(at_ref, w_ref, own_ref, other_ref, high_ref, low_ref, edge_ref, p_ref, x_ref):
+    chips, _, block, tile = own_ref.shape
+    column_groups, row_groups = 2 * chips, 16
+    size = 256
+    core = at_ref[1] % 2
+    for ref, side in ((own_ref, core), (other_ref, 1 - core)):
+        for c in range(chips):
+            for p in range(2):
+                lo = pl.multiple_of(p * NB + (2 * c + side) * block, block)
+                p_ref[pl.ds(lo, block), :] = ref[c, p]
     for i in range(0, WIDE, size):
-        z = mm(w_ref[i : i + size, : i + size], a_ref[: i + size, :])
-        high_ref[i : i + size, :], low_ref[i : i + size, :] = split(z)
-        y_ref[i : i + size, :] = z[:, wide - 128 :]
-
-
-def column_part(w, gathered):
+        x = mm(w_ref[i : i + size, : i + size], p_ref[: i + size, :])
+        x_ref[i : i + size, :] = x
+        high_ref[:, i : i + size], low_ref[:, i : i + size] = split(x.T)
+    mine = pl.multiple_of(at_ref[1] * block, block)
+    edge = jnp.concatenate([x_ref[pl.ds(mine, block), :], x_ref[pl.ds(NB + mine, block), :]], axis=0).T
+    local = lax.broadcasted_iota(jnp.int32, (tile, 1), 0) + pl.program_id(0) * tile
+    rows = (local // block * row_groups + at_ref[0]) * block + local % block
+    lane = lax.broadcasted_iota(jnp.int32, (1, 2 * block), 1)
+    lanes = (lane // block * column_groups + at_ref[1]) * block + lane % block
+    edge_ref[:, : 2 * block] = jnp.where(rows >= lanes, edge, 0.0)
+
+
+def panel_part(at, w, own, other):
     vmem = pl.BlockSpec(memory_space=pltpu.VMEM)
-    wide = gathered.shape[2]
+    tile = 256
+    chips, _, block, local_rows = own.shape
+    halves = pl.BlockSpec((chips, 2, block, tile), lambda i: (0, 0, 0, i))
     return pl.pallas_call(
-        column_kernel,
+        panel_kernel,
+        grid=(local_rows // tile,),
         out_shape=(
-            jax.ShapeDtypeStruct((WIDE, wide), BF16),
-            jax.ShapeDtypeStruct((WIDE, wide), BF16),
-            jax.ShapeDtypeStruct((WIDE, 128), F32),
+            jax.ShapeDtypeStruct((local_rows, WIDE), BF16),
+            jax.ShapeDtypeStruct((local_rows, WIDE), BF16),
+            jax.ShapeDtypeStruct((local_rows, 128), F32),
         ),
-        in_specs=[vmem, vmem],
-        out_specs=(vmem, vmem, vmem),
-        scratch_shapes=[pltpu.VMEM((WIDE, wide), F32)],
-        compiler_params=pltpu.CompilerParams(vmem_limit_bytes=24 << 20),
-        cost_estimate=pl.CostEstimate(flops=6_000_000_000, bytes_accessed=8 << 20, transcendentals=0),
-        name="column_part",
-    )(w, gathered)
-
-
-def row_kernel(at_ref, w_ref, high_ref, low_ref, g_ref, cov_ref, field_ref, out_ref, fout_ref, p_ref, x_ref):
-    column_groups, _, block, tile = g_ref.shape
-    row_groups = 16
-    columns = cov_ref.shape[1]
+        in_specs=[pl.BlockSpec(memory_space=pltpu.SMEM), vmem, halves, halves],
+        out_specs=(
+            pl.BlockSpec((tile, WIDE), lambda i: (i, 0)),
+            pl.BlockSpec((tile, WIDE), lambda i: (i, 0)),
+            pl.BlockSpec((tile, 128), lambda i: (i, 0)),
+        ),
+        scratch_shapes=[pltpu.VMEM((WIDE, tile), F32), pltpu.VMEM((WIDE, tile), F32)],
+        compiler_params=pltpu.CompilerParams(vmem_limit_bytes=16 << 20),
+        cost_estimate=pl.CostEstimate(flops=8_000_000_000, bytes_accessed=12 << 20, transcendentals=0),
+        name="panel_part",
+    )(at, w, own, other)
+
+
+def update_kernel(
+    at_ref, w_ref, high_ref, low_ref, edge_ref, cov_ref, field_ref, g_ref, out_ref, fout_ref, a_ref, b_ref, zh_ref, zl_ref, y_ref, sem
+):
+    quarters, row_groups, block, wide = a_ref.shape
+    tile, columns = cov_ref.shape
     width = field_ref.shape[0]
-    size = 256
+    size = row_groups * block
     own = 2 * block
-    for p in range(2):
-        p_ref[p * NB : (p + 1) * NB, :] = g_ref[:, p].reshape(NB, tile)
-    for i in range(0, WIDE, size):
-        x_ref[i : i + size, :] = mm(w_ref[i : i + size, : i + size], p_ref[: i + size, :])
-    x_high, x_low = split(x_ref[...].T)
-    z_high, z_low = high_ref[...], low_ref[...]
+    step = pl.program_id(0)
+
+    @pl.when(step == 0)
+    def _():
+        copies = []
+        for q in range(quarters):
+            hi = (q + 1) * size
+            copies.append(pltpu.make_async_copy(g_ref.at[:, pl.ds(q * block, block), :], a_ref.at[q], sem.at[0, q]))
+            copies.append(pltpu.make_async_copy(w_ref.at[pl.ds(q * size, size), :hi], b_ref.at[q, :, :hi], sem.at[1, q]))
+        for copy in copies:
+            copy.start()
+        for q in range(quarters):
+            copies[2 * q].wait()
+            copies[2 * q + 1].wait()
+            lo, hi = q * size, (q + 1) * size
+            z = mm(b_ref[q, :, :hi], a_ref[: q + 1].reshape(hi, wide))
+            zh_ref[lo:hi, :], zl_ref[lo:hi, :] = split(z)
+            y_ref[lo:hi, :] = z[:, columns:]
 
     def dot(a, b):
         return jnp.dot(a, b, preferred_element_type=F32)
 
+    x_high, x_low = high_ref[...], low_ref[...]
+    z_high, z_low = zh_ref[...], zl_ref[...]
     change = dot(x_high, z_high) + (dot(x_high, z_low) + dot(x_low, z_high))
-    local = lax.broadcasted_iota(jnp.int32, (tile, 1), 0) + pl.program_id(0) * tile
+    local = lax.broadcasted_iota(jnp.int32, (tile, 1), 0) + step * tile
     rows = (local // block * row_groups + at_ref[0]) * block + local % block
-    mine = pl.multiple_of(at_ref[1] * block, block)
-    edge = jnp.concatenate([x_ref[pl.ds(mine, block), :], x_ref[pl.ds(NB + mine, block), :]], axis=0).T
-    lane = lax.broadcasted_iota(jnp.int32, (1, own), 1)
-    lanes = (lane // block * column_groups + at_ref[1]) * block + lane % block
     out_ref[...] = jnp.where(rows < WIDE, 0.0, cov_ref[...] - change[:, :columns])
-    out_ref[:, :own] = jnp.where(rows >= lanes, edge, 0.0)
+    out_ref[:, :own] = edge_ref[:, :own]
     fout_ref[...] = field_ref[...] - change[:, columns:].T[:width]
 
-
-def row_part(at, w, high, low, gathered, covariance, fields):
-    vmem = pl.BlockSpec(memory_space=pltpu.VMEM)
+    @pl.when(step == 0)
+    def _():
+        mine = [y_ref[pl.ds(pl.multiple_of(q * size + at_ref[0] * block, block), block), :] for q in range(quarters)]
+        fout_ref[:, : quarters * block] = jnp.concatenate(mine, axis=0).T[:width]
+
+
+def update_part(at, w, high, low, edge, covariance, fields, gathered):
     tile = 256
-    groups, _, block, local_rows = gathered.shape
-    columns = covariance.shape[1]
+    row_groups, top, wide = gathered.shape
+    local_rows, columns = covariance.shape
     width = fields.shape[0]
+    quarters = WIDE // 256
+    block = top // quarters
+    by_rows = lambda i: (i, 0)
     return pl.pallas_call(
-        row_kernel,
+        update_kernel,
         grid=(local_rows // tile,),
         out_shape=(
             jax.ShapeDtypeStruct(covariance.shape, F32),
@@ -234,22 +270,30 @@
         ),
         in_specs=[
             pl.BlockSpec(memory_space=pltpu.SMEM),
-            vmem,
-            vmem,
-            vmem,
-            pl.BlockSpec((groups, 2, block, tile), lambda i: (0, 0, 0, i)),
-            pl.BlockSpec((tile, columns), lambda i: (i, 0)),
+            pl.BlockSpec(memory_space=pltpu.HBM),
+            pl.BlockSpec((tile, WIDE), by_rows),
+            pl.BlockSpec((tile, WIDE), by_rows),
+            pl.BlockSpec((tile, 128), by_rows),
+            pl.BlockSpec((tile, columns), by_rows),
             pl.BlockSpec((width, tile), lambda i: (0, i)),
+            pl.BlockSpec(memory_space=pltpu.HBM),
         ],
         out_specs=(
-            pl.BlockSpec((tile, columns), lambda i: (i, 0)),
+            pl.BlockSpec((tile, columns), by_rows),
             pl.BlockSpec((width, tile), lambda i: (0, i)),
         ),
-        scratch_shapes=[pltpu.VMEM((WIDE, tile), F32), pltpu.VMEM((WIDE, tile), F32)],
-        compiler_params=pltpu.CompilerParams(vmem_limit_bytes=40 << 20),
-        cost_estimate=pl.CostEstimate(flops=12_000_000_000, bytes_accessed=16 << 20, transcendentals=0),
-        name="row_part",
-    )(at, w, high, low, gathered, covariance, fields)
+        scratch_shapes=[
+            pltpu.VMEM((quarters, row_groups, block, wide), F32),
+            pltpu.VMEM((quarters, 256, WIDE), F32),
+            pltpu.VMEM((WIDE, wide), BF16),
+            pltpu.VMEM((WIDE, wide), BF16),
+            pltpu.VMEM((WIDE, wide - columns), F32),
+            pltpu.SemaphoreType.DMA((2, quarters)),
+        ],
+        compiler_params=pltpu.CompilerParams(vmem_limit_bytes=62 << 20),
+        cost_estimate=pl.CostEstimate(flops=9_000_000_000, bytes_accessed=16 << 20, transcendentals=0),
+        name="update_part",
+    )(at, w, high, low, edge, covariance, fields, gathered)
 
 
 def spread_out(piece, axis, count, groups=None):
@@ -257,16 +301,10 @@
     return lax.all_to_all(copies, axis, 0, 0, axis_index_groups=groups, tiled=True)
 
 
-def finish(at, covariance, fields, own_pieces, other_pieces, panel, across):
-    width = fields.shape[0]
+def finish(at, covariance, fields, own_pieces, other_pieces, own_panel, other_panel, across):
     w = inverse_factor(at, own_pieces, other_pieces)
-    high, low, y = column_part(w, across)
-    factored, moved = row_part(at, w, high, low, panel, covariance, fields)
-    row_groups, top, _ = across.shape
-    block = WIDE // row_groups // (top // 16)
-    solved = y.reshape(top // block, row_groups, block, 128)
-    solved = lax.dynamic_index_in_dim(solved, at[0], 1, keepdims=False).reshape(top, 128)[:, :width]
-    return (factored, moved.at[:, :top].set(solved.T))
+    high, low, edge = panel_part(at, w, own_panel, other_panel)
+    return update_part(at, w, high, low, edge, covariance, fields, across)
 
 
 def shards(covariance, fields):
@@ -280,21 +318,27 @@
     own = 2 * block
     quarters = top // block
     cores = 2
+    same_core = [[cores * i + k for i in range(cols_n // cores)] for k in range(cores)]
+    partner = [(i, i ^ 1) for i in range(cols_n)]
 
     corner = covariance[:top, :own]
     packed = jnp.concatenate([corner[q * block : (q + 1) * block] for q in range(quarters)], axis=1)
+    panel = covariance[:, :own].T.reshape(2, block, local_rows)
+    own_panel = lax.all_gather(panel, "col", axis=0, axis_index_groups=same_core)
+
     tall = spread_out(packed, "row", rows_n).reshape(rows_n * block, quarters * own).T
     strip = jnp.concatenate([tall[q * own : (q + 1) * own] for q in range(quarters)], axis=1)
     strip = jnp.concatenate([strip[:block], strip[block:, NB:]], axis=1)
-    same_core = [[cores * i + k for i in range(cols_n // cores)] for k in range(cores)]
+
+    across = jnp.concatenate([covariance[:top], jnp.pad(fields[:, :top].T, ((0, 0), (0, 128 - width)))], axis=1)
+    across, strip = lax.optimization_barrier((across, strip))
+    across = lax.all_gather(across, "row", axis=0)
+
     own_pieces = spread_out(strip, "col", cols_n // cores, same_core)
-    other_pieces = lax.ppermute(own_pieces, "col", [(i, i ^ 1) for i in range(cols_n)])
-
-    across = jnp.concatenate([covariance[:top], jnp.pad(fields[:, :top].T, ((0, 0), (0, 128 - width)))], axis=1)
-    across = lax.all_gather(across, "row", axis=0)
-    panel = covariance[:, :own].T.reshape(2, block, local_rows)
-    panel = lax.all_gather(panel, "col", axis=0)
-    return finish(at, covariance, fields, own_pieces, other_pieces, panel, across)
+    own_pieces, own_panel = lax.optimization_barrier((own_pieces, own_panel))
+    other_pieces = lax.ppermute(own_pieces, "col", partner)
+    other_panel = lax.ppermute(own_panel, "col", partner)
+    return finish(at, covariance, fields, own_pieces, other_pieces, own_panel, other_panel, across)
 
 
 def solution(mesh):

time: 190 us -> 185 us (0.974)
  the two profiles are of different devices: /device:TPU:1 before, /device:TPU:2 now
where the time goes in v2:
time: 185 us
  Pallas kernels  82.1 us (44%)
  waiting for transfers between devices  32.1 us (17%)
  blocking collectives  25.7 us (14%)
  starting transfers between devices  19.6 us (11%)
  between operations  14.2 us (8%)
  local copies, waits for them, and re-layouts  10.2 us (6%)
    pallas_call x1, Pallas kernels, inverse_factor(): pl.pallas_call(factor_kernel, out_shape=jax.ShapeDtypeStruct((WIDE, WIDE)...  50.4 us
    all_to_all x1, blocking collectives, spread_out(): lax.all_to_all(copies, axis, 0, 0, axis_index_groups=groups, tiled=True)  25.7 us
    pallas_call x1, Pallas kernels, update_part(): pl.pallas_call(update_kernel, grid=(local_rows // tile,), out_shape=(jax....  18.8 us
    all_gather x1, waiting for transfers between devices, shards(): lax.all_gather(panel, 'col', axis=0, axis_index_groups=same_core)  15.2 us
    all_to_all x1, starting transfers between devices, spread_out(): lax.all_to_all(copies, axis, 0, 0, axis_index_groups=groups, tiled=True)  15.2 us
    all_to_all x1, waiting for transfers between devices, spread_out(): lax.all_to_all(copies, axis, 0, 0, axis_index_groups=groups, tiled=True)  13.3 us
    pallas_call x1, Pallas kernels, panel_part(): pl.pallas_call(panel_kernel, grid=(local_rows // tile,), out_shape=(jax.S...  12.9 us
    unnamed x13, local copies, waits for them, and re-layouts  5.53 us
  transfers between devices with their start and end apart: 5, of which 4 were waited for; matrix products, arithmetic and copies ran while one was open for 2% of the time, Pallas kernels for 34%

profile of v2, /device:TPU:2, one launch (start us, length us, event | category | flops | bytes accessed | tf_op | source)
XLA Modules:
  0.0 184.7 jit_solution(4411132717811132867)
XLA Ops:
  7.2 0.0 slice-start
  7.2 0.0 all-gather.4.cloned.1.call-start
  7.2 1.1 slice_bitcast_fusion
  8.3 0.8 copy.17
  9.2 0.0 all-gather.4.cloned.1.call-update
  9.2 0.8 fusion.1
  9.9 0.1 pad_maximum_fusion.4
  10.0 0.7 broadcast_in_dim.4
  10.7 15.2 %all-to-all-start = ((f32[16,16,128]{2,1,0:T(8,128)}), f32[16,16,128]{2,1,0:T(8,128)S(1)}, u32[]{:S(2)}, u32[]{:S(2)}) async-start(f32[16,16,128]{2,1,0:T(8,128)} %broadcast_in_dim.4), calls=%async_computation | async-start | bytes 262144 | tf_op jit(solution)/shard_map/all_to_all | solution.py:301
  25.9 0.0 all-gather.6.cloned.1.call-start
  25.9 0.7 slice_bitcast_fusion.1
  26.6 0.1 copy.18
  26.7 0.0 slice-done
  26.7 0.7 select_maximum_fusion
  27.4 13.3 %all-to-all-done = f32[16,16,128]{2,1,0:T(8,128)S(1)} async-done(((f32[16,16,128]{2,1,0:T(8,128)}), f32[16,16,128]{2,1,0:T(8,128)S(1)}, u32[]{:S(2)}, u32[]{:S(2)}) %all-to-all-start) | async-done | bytes 131104 | tf_op jit(solution)/shard_map/all_to_all | solution.py:301
  40.7 0.2 fusion.2
  40.8 0.1 copy.11
  40.9 0.1 copy.12
  41.0 0.1 copy.13
  41.1 0.1 copy.14
  41.2 0.0 all-gather.6.cloned.1.call-update
  41.2 0.2 broadcast_in_dim.5
  41.4 25.7 %all_to_all.10.own_ref = f32[16,16,1536]{2,1,0:T(8,128)S(1)} all-to-all(f32[16,16,1536]{2,1,0:T(8,128)S(1)} %broadcast_in_dim.5), channel_id=1, replica_groups={{0,2,4,6,8,10,12,14,16,18,20,22,24,26,28,30},{1,3,5,7,9,11,13,15,17,19,..., dimensions={0} | all-to-all | bytes 3145728 | tf_op jit(solution)/shard_map/all_to_all | solution.py:301
  67.0 15.2 %all-gather.4.cloned.1.call-done.own_ref = f32[16,2,16,1024]{3,2,1,0:T(8,128)} async-done(((f32[1,2,16,1024]{3,2,1,0:T(8,128)}), f32[16,2,16,1024]{3,2,1,0:T(8,128)}) %all-gather.4.cloned.1.call-update) | async-done | bytes 2097168 | tf_op jit(solution)/shard_map/all_gather | solution.py:327
  82.3 1.9 %collective-permute-start = (f32[16,16,1536]{2,1,0:T(8,128)S(1)}, f32[16,16,1536]{2,1,0:T(8,128)S(1)}, u32[]{:S(2)}, u32[]{:S(2)}) collective-permute-start(f32[16,16,1536]{2,1,0:T(8,128)S(1)} %all_to_all.10.own_ref), channel_id=1, source_target_pairs={{0,1},{1,0},{2,3},{3,2},{4,5},{5,4},{6,7},{7,6},{8,9},{9,8},{10,11... | collective-permute-start | bytes 4718600 | tf_op jit(solution)/shard_map/ppermute | solution.py:339
  84.2 2.4 %collective-permute-start.1 = (f32[16,2,16,1024]{3,2,1,0:T(8,128)}, f32[16,2,16,1024]{3,2,1,0:T(8,128)}, u32[]{:S(2)}, u32[]{:S(2)}) collective-permute-start(f32[16,2,16,1024]{3,2,1,0:T(8,128)} %all-gather.4.cloned.1.call-done.own_ref), channel_id=1, source_target_pairs={{0,1},{1,0},{2,3},{3,2},{4,5},{5,4},{6,7},{7,6},{8,9},{9,8},{10,11... | collective-permute-start | bytes 6291464 | tf_op jit(solution)/shard_map/ppermute | solution.py:340
  86.6 0.1 pad_add_fusion.at_ref
  86.7 0.0 copy-start.1
  86.7 0.0 copy-start
  86.7 0.9 collective-permute-done.other_ref
  87.6 50.4 %inverse_factor.1.w_ref = f32[1024,1024]{1,0:T(8,128)S(1)} custom-call(s32[2]{0:T(128)S(1)} %pad_add_fusion.at_ref, f32[16,16,1536]{2,1,0:T(8,128)S(1)} %all_to_all.10.own_ref, f32[16,16,1536]{2,1,0:T(8,128)S(1)} %collective-permute-done.other_ref), custom_call_target="tpu_custom_call" | custom-call | flops 8000000000 | bytes 8388608 | tf_op jit(solution)/shard_map/inverse_factor/pallas_call | solution.py:145
  138.0 0.0 collective-permute-done.1.other_ref
  138.0 0.0 copy-done.1
  138.0 0.0 copy-done
  138.0 12.9 %panel_part.1 = (bf16[1024,1024]{1,0:T(8,128)(2,1)S(1)}, bf16[1024,1024]{1,0:T(8,128)(2,1)S(1)}, f32[1024,128]{1,0:T(8,128)S(1)}) custom-call(s32[2]{0:T(128)S(1)} %pad_add_fusion.at_ref, f32[1024,1024]{1,0:T(8,128)S(1)} %inverse_factor.1.w_ref, f32[16,2,16,1024]{3,2,1,0:T(8,128)S(1)} %copy-done, f32[16,2,16,1024]{3,2,1,0:T(8,128)} %collective-permute-done.1.other_ref), custom_call_target="tpu_custom_call" | custom-call | flops 8000000000 | bytes 12582912 | tf_op jit(solution)/shard_map/panel_part/pallas_call | solution.py:190
  150.9 0.0 copy-start.2
  150.9 1.9 %copy-done.2 = f32[1024,1024]{1,0:T(8,128)} copy-done((f32[1024,1024]{1,0:T(8,128)}, f32[1024,1024]{1,0:T(8,128)S(1)}, u32[]{:S(2)}) %copy-start.2) | copy-done | bytes 4194328
  152.9 0.0 copy-start.3
  152.9 1.4 copy-done.3
  154.3 0.0 copy-start.4
  154.3 1.3 copy-done.4
  155.6 0.0 copy-start.5
  155.6 0.8 copy-done.5
  156.4 2.7 %all-gather.6.cloned.1.call-done = f32[1024,640]{1,0:T(8,128)} async-done(((f32[64,640]{1,0:T(8,128)}), f32[1024,640]{1,0:T(8,128)}) %all-gather.6.cloned.1.call-update) | async-done | bytes 2621456 | tf_op jit(solution)/shard_map/all_gather | solution.py:335
  159.1 18.8 %update_part.1 = (f32[1024,512]{1,0:T(8,128)}, f32[16,1024]{1,0:T(8,128)}) custom-call(s32[2]{0:T(128)} %copy-done.1, f32[1024,1024]{1,0:T(8,128)} %copy-done.2, bf16[1024,1024]{1,0:T(8,128)(2,1)} %copy-done.3, bf16[1024,1024]{1,0:T(8,128)(2,1)} %copy-done.4, f32[1024,128]{1,0:T(8,128)} %copy-done.5, f32[1024,512]{1,0:T(8,128)} %cov_ref.1, ...), custom_call_target="tpu_custom_call" | custom-call | flops 8999999488 | bytes 16777216 | tf_op jit(solution)/shard_map/update_part/pallas_call | solution.py:264
  (1 shorter events, 0.0 us)
Async XLA Ops:
  7.2 19.6 %slice-start = ((f32[1024,512]{1,0:T(8,128)}), f32[64,512]{1,0:T(8,128)S(1)}, s32[]{:S(2)}) async-start(f32[1024,512]{1,0:T(8,128)} %cov_ref.1), calls=%async_computation.4 | async-start | bytes 262144 | tf_op jit(solution)/shard_map/slice | solution.py:333
  7.2 75.1 %all-gather.4.cloned.1.call-start = ((), (), s32[]{:S(2)}) async-start(), calls=%async_computation.2 | async-start | bytes 2228224 | tf_op jit(solution)/shard_map/all_gather | solution.py:327
  10.7 30.0 %all-to-all-start = ((f32[16,16,128]{2,1,0:T(8,128)}), f32[16,16,128]{2,1,0:T(8,128)S(1)}, u32[]{:S(2)}, u32[]{:S(2)}) async-start(f32[16,16,128]{2,1,0:T(8,128)} %broadcast_in_dim.4), calls=%async_computation | async-start | bytes 262144 | tf_op jit(solution)/shard_map/all_to_all | solution.py:301
  25.9 133.2 %all-gather.6.cloned.1.call-start = ((), (), s32[]{:S(2)}) async-start(), calls=%async_computation.3 | async-start | bytes 2785280 | tf_op jit(solution)/shard_map/all_gather | solution.py:335
  82.3 5.3 %collective-permute-start = (f32[16,16,1536]{2,1,0:T(8,128)S(1)}, f32[16,16,1536]{2,1,0:T(8,128)S(1)}, u32[]{:S(2)}, u32[]{:S(2)}) collective-permute-start(f32[16,16,1536]{2,1,0:T(8,128)S(1)} %all_to_all.10.own_ref), channel_id=1, source_target_pairs={{0,1},{1,0},{2,3},{3,2},{4,5},{5,4},{6,7},{7,6},{8,9},{9,8},{10,11... | collective-permute-start | bytes 4718600 | tf_op jit(solution)/shard_map/ppermute | solution.py:339
  84.2 53.8 %collective-permute-start.1 = (f32[16,2,16,1024]{3,2,1,0:T(8,128)}, f32[16,2,16,1024]{3,2,1,0:T(8,128)}, u32[]{:S(2)}, u32[]{:S(2)}) collective-permute-start(f32[16,2,16,1024]{3,2,1,0:T(8,128)} %all-gather.4.cloned.1.call-done.own_ref), channel_id=1, source_target_pairs={{0,1},{1,0},{2,3},{3,2},{4,5},{5,4},{6,7},{7,6},{8,9},{9,8},{10,11... | collective-permute-start | bytes 6291464 | tf_op jit(solution)/shard_map/ppermute | solution.py:340
  86.7 51.3 %copy-start.1 = (s32[2]{0:T(128)}, s32[2]{0:T(128)S(1)}, u32[]{:S(2)}) copy-start(s32[2]{0:T(128)S(1)} %pad_add_fusion.at_ref) | copy-start | bytes 28
  86.7 51.3 %copy-start = (f32[16,2,16,1024]{3,2,1,0:T(8,128)S(1)}, f32[16,2,16,1024]{3,2,1,0:T(8,128)}, u32[]{:S(2)}) copy-start(f32[16,2,16,1024]{3,2,1,0:T(8,128)} %all-gather.4.cloned.1.call-done.own_ref) | copy-start | bytes 6291460
  150.9 1.9 %copy-start.2 = (f32[1024,1024]{1,0:T(8,128)}, f32[1024,1024]{1,0:T(8,128)S(1)}, u32[]{:S(2)}) copy-start(f32[1024,1024]{1,0:T(8,128)S(1)} %inverse_factor.1.w_ref) | copy-start | bytes 12582916
  152.9 1.4 copy-start.3
  154.3 1.3 copy-start.4
  155.6 0.8 copy-start.5
Sparse Core Ops, SparseCore 0:
  11.0 71.2 all-gather.3
  84.9 74.1 all-gather.5
